TPU v7x, 128 devices: a whole 4x4x4 slice. The times are simulated.
128 devices in a mesh: grp: 2 (over y_lo), sp: 64 (over x, y_hi, z, core).
Axes of the slice: x: 4, y: 4 (y_hi: 2, y_lo: 2; y = y_hi * 2 + y_lo), z: 4, core: 2. Of those that a mesh axis runs over, the one named last changes fastest.
Arguments:
- modes: bfloat16 [3, 512, 32, 16, 256], P(None, 'sp', 'grp'), may hold values from -16 to 16
- convecting: int32 [12], replicated, may hold values from 0 to 255, as said below
Outputs:
- skew_tensor: float32 [12, 256, 256], P(None, 'sp')
Inputs may be any that keep to these rules, and one draw needn't show every extreme that they name: `convecting`: 12 distinct mode indices.
All inputs are finite; a program needn't handle non-finite values.
Results may differ from a plain program's by a relative error of at most 0.0029.
Values may be sent and summed in bfloat16 or wider, within the bound.
No kernel may reach another device: no remote copies, remote signals or barrier semaphores. Data moves between devices by JAX's collectives and lax.ppermute only.
A program may use at most 64 MiB of HBM per device.

v0:
```python
import math
import jax
import jax.numpy as jnp
from jax import lax
from jax.sharding import PartitionSpec as P


def extended(block, sides, width):
    for axis, dim in sides:
        count = lax.axis_size(axis)
        forward = [(i, i + 1) for i in range(count - 1)]
        forward.append((count - 1, 0))
        backward = [(target, source) for source, target in forward]
        low = lax.ppermute(
            lax.slice_in_dim(block, block.shape[dim] - width, None, axis=dim), axis, forward
        )
        high = lax.ppermute(lax.slice_in_dim(block, 0, width, axis=dim), axis, backward)
        block = jnp.concatenate([low, block, high], axis=dim)
    return block


def shards(modes, convecting):
    n_sp = lax.axis_size("sp")
    n_grp = lax.axis_size("grp")
    width = modes.shape[4]
    cells = modes.shape[1] * n_sp * modes.shape[2] * n_grp * modes.shape[3]
    padded = extended(modes, (("grp", 2), ("sp", 1)), 1)
    picker = (jnp.arange(width, dtype=jnp.int32)[:, None] == convecting[None, :]).astype(
        jnp.bfloat16
    )
    velocity = jnp.einsum("cxyzm,ms->scxyz", modes, picker, preferred_element_type=jnp.float32)
    test_flat = modes.reshape(-1, width)

    def project(carry, field):
        centre = padded[:, 1:-1, 1:-1].astype(jnp.float32)
        along_x = padded[:, 2:, 1:-1].astype(jnp.float32) - padded[:, :-2, 1:-1].astype(jnp.float32)
        along_y = padded[:, 1:-1, 2:].astype(jnp.float32) - padded[:, 1:-1, :-2].astype(jnp.float32)
        along_z = jnp.roll(centre, -1, axis=3) - jnp.roll(centre, 1, axis=3)
        moved = 0.5 * (
            field[0][..., None] * along_x
            + field[1][..., None] * along_y
            + field[2][..., None] * along_z
        )
        moved = moved.astype(jnp.bfloat16).reshape(-1, width)
        block = lax.dot_general(
            test_flat, moved, (((0,), (0,)), ((), ())), preferred_element_type=jnp.float32
        )
        return (carry, block)

    _, stacked = lax.scan(project, jnp.zeros((), jnp.float32), velocity)
    mine = lax.psum_scatter(stacked, "sp", scatter_dimension=1, tiled=True)
    owned = lax.psum(mine, "grp")
    owned = owned / math.sqrt(cells)
    mirrored = lax.all_to_all(owned, "sp", split_axis=2, concat_axis=1, tiled=True)
    return 0.5 * (owned - jnp.swapaxes(mirrored, 1, 2))


def solution(mesh):
    placed = (P(None, "sp", "grp", None, None), P())
    return jax.shard_map(
        shards, mesh=mesh, in_specs=placed, out_specs=P(None, "sp", None), check_vma=False
    )
```

profile of v0, /device:TPU:1, one launch (start us, length us, event | category | flops | bytes accessed | tf_op | source)
XLA Modules:
  0.0 910.7 jit_solution(5108024089505814859)
XLA Ops:
  7.6 2.2 collective-permute-start
  9.9 4.2 collective-permute-done
  14.1 2.3 constant_dynamic-update-slice_fusion.2
  16.4 1.8 collective-permute-done.1
  18.3 1.7 copy-done.1
  21.0 3.3 collective-permute-start.2
  24.3 5.6 fusion.6
  29.9 2.7 collective-permute-done.3
  32.7 3.4 pad_maximum_fusion
  36.1 183.5 %while.10 = (s32[]{:T(128)}, f32[12,256,256]{2,1,0:T(8,128)}, f32[12,3,8,16,16]{4,0,3,2,1:T(8,128)}, bf16[3,10,18,16,256]{4,3,2,1,0:T(8,128)(2,1)}, bf16[3,8,18,...) while((s32[]{:T(128)}, f32[12,256,256]{2,1,0:T(8,128)}, ...), condition=%wide.region_1.2_spmd, body=%wide.region_0.1_spmd.sunk | while | flops 830472192 | bytes 61203032 | solution.py:50
  36.1 1.6 constant_dynamic-slice_fusion.3
  37.6 1.9 fusion.24
  40.4 7.4 fusion.25
  47.8 1.7 convolution_bitcast_fusion.2
  49.5 1.1 copy.35
  51.4 1.5 constant_dynamic-slice_fusion.3
  52.9 1.9 fusion.24
  55.7 7.4 fusion.25
  63.1 1.7 convolution_bitcast_fusion.2
  64.8 1.1 copy.35
  66.6 1.5 constant_dynamic-slice_fusion.3
  68.2 1.9 fusion.24
  71.0 7.4 fusion.25
  78.4 1.7 convolution_bitcast_fusion.2
  80.1 1.1 copy.35
  81.9 1.5 constant_dynamic-slice_fusion.3
  83.5 1.9 fusion.24
  86.3 7.4 fusion.25
  93.7 1.7 convolution_bitcast_fusion.2
  97.2 1.5 constant_dynamic-slice_fusion.3
  98.8 1.9 fusion.24
  101.6 7.4 fusion.25
  109.0 1.7 convolution_bitcast_fusion.2
  112.5 1.5 constant_dynamic-slice_fusion.3
  114.1 1.9 fusion.24
  116.9 7.4 fusion.25
  124.3 1.7 convolution_bitcast_fusion.2
  127.8 1.5 constant_dynamic-slice_fusion.3
  129.4 1.9 fusion.24
  132.2 7.4 fusion.25
  139.6 1.7 convolution_bitcast_fusion.2
  143.1 1.5 constant_dynamic-slice_fusion.3
  144.7 1.9 fusion.24
  147.5 7.4 fusion.25
  154.9 1.7 convolution_bitcast_fusion.2
  158.4 1.5 constant_dynamic-slice_fusion.3
  160.0 1.9 fusion.24
  162.8 7.4 fusion.25
  170.2 1.7 convolution_bitcast_fusion.2
  173.7 1.5 constant_dynamic-slice_fusion.3
  175.3 1.9 fusion.24
  178.1 7.4 fusion.25
  185.5 1.7 convolution_bitcast_fusion.2
  189.0 1.5 constant_dynamic-slice_fusion.3
  190.6 1.9 fusion.24
  193.3 7.4 fusion.25
  200.7 1.7 convolution_bitcast_fusion.2
  204.3 1.5 constant_dynamic-slice_fusion.3
  205.8 1.9 fusion.24
  208.6 7.4 fusion.25
  216.0 1.7 convolution_bitcast_fusion.2
  220.8 651.3 %all-reduce.3.cloned.1.call-done = f32[12,256,256]{2,1,0:T(8,128)} async-done(((f32[12,256,256]{2,1,0:T(8,128)}), f32[12,256,256]{2,1,0:T(8,128)}) %all-reduce.3.cloned.1.call-update) | async-done | bytes 3145744
  873.0 5.7 psum.7
  879.6 21.0 %all_to_all.18 = f32[64,1,192]{2,1,0:T(1,128)S(1)} all-to-all(f32[64,1,192]{2,1,0:T(1,128)S(1)} %reshape.21), channel_id=1, replica_groups=mesh['grp'=2,'sp'=64] {'sp'}, dimensions={0} | all-to-all | bytes 98304 | tf_op jit(solution)/shard_map/all_to_all | solution.py:54
  (76 shorter events, 36.5 us)
Async XLA Ops:
  6.5 865.5 %all-reduce.3.cloned.1.call-start = ((), (), s32[]{:S(2)}) async-start(), calls=%async_computation.1 | async-start | bytes 6291456
  7.6 6.5 collective-permute-start
  9.8 8.5 collective-permute-start.1
  14.1 10.2 %copy-start = (bf16[3,8,16,16,256]{4,3,2,1,0:T(8,128)(2,1)S(1)}, bf16[3,8,16,16,256]{4,3,2,1,0:T(8,128)(2,1)}, u32[]{:S(2)}) copy-start(bf16[3,8,16,16,256]{4,3,2,1,0:T(8,128)(2,1)} %param.4) | copy-start | bytes 9437188
  14.1 10.2 %copy-start.3 = (s32[12]{0:T(128)S(1)}, s32[12]{0:T(128)}, u32[]{:S(2)}) copy-start(s32[12]{0:T(128)} %param.5) | copy-start | bytes 148
  18.3 1.8 copy-start.1
  21.0 8.9 collective-permute-start.2
  24.3 8.3 collective-permute-start.3
  24.3 8.3 copy-start.2
  36.1 183.5 %copy-start.4 = (u32[128]{0:T(128)S(1)}, u32[128]{0:T(128)}, u32[]{:S(2)}) copy-start(u32[128]{0:T(128)} %constant.23) | copy-start | bytes 1540
Sparse Core Ops, SparseCore 0:
  219.7 652.3 all-reduce.2
where the time goes:
time: 912 us; the launch traced here: 911 us
  waiting for transfers between devices  660 us (72%)
  other arithmetic  93.7 us (10%)
  local copies, waits for them, and re-layouts  83.7 us (9%)
  blocking collectives  26.7 us (3%)
  matrix products  26.2 us (3%)
  between operations  14.2 us (2%)
    unnamed x2, waiting for transfers between devices  651 us
    convert_element_type x12, other arithmetic, project(): moved = moved.astype(jnp.bfloat16).reshape(-1, width)  88.8 us
    slice x24, local copies, waits for them, and re-layouts, project(): along_z = jnp.roll(centre, -1, axis=3) - jnp.roll(centre, 1, axis=3)  33.1 us
    dynamic_update_slice x24, local copies, waits for them, and re-layouts, shards(): _, stacked = lax.scan(project, jnp.zeros((), jnp.float32), velocity)  21.6 us
    all_to_all x1, blocking collectives, shards(): lax.all_to_all(owned, 'sp', split_axis=2, concat_axis=1, tiled=True)  21 us
    dot_general x12, matrix products, project(): lax.dot_general(test_flat, moved, (((0,), (0,)), ((), ())), preferred_ele...  20.6 us
    dynamic_slice x12, local copies, waits for them, and re-layouts, shards(): _, stacked = lax.scan(project, jnp.zeros((), jnp.float32), velocity)  18.6 us
  transfers between devices with their start and end apart: 5, of which 4 were waited for; matrix products, arithmetic and copies ran while one was open for 1% of the time, Pallas kernels for 0%

commit v1 on v0

--- a/solution.py
+++ b/solution.py
@@ -3,6 +3,16 @@
 import jax.numpy as jnp
 from jax import lax
 from jax.sharding import PartitionSpec as P
+
+see_vectors_by_axis = lambda m: jnp.concatenate(
+    lax.all_to_all(
+        jnp.stack(jnp.split(m, lax.axis_size("sp"), axis=2), axis=0),
+        concat_axis=0,
+        split_axis=0,
+        axis_name="sp",
+    ),
+    axis=1,
+)
 
 
 def extended(block, sides, width):
@@ -51,7 +61,7 @@
     mine = lax.psum_scatter(stacked, "sp", scatter_dimension=1, tiled=True)
     owned = lax.psum(mine, "grp")
     owned = owned / math.sqrt(cells)
-    mirrored = lax.all_to_all(owned, "sp", split_axis=2, concat_axis=1, tiled=True)
+    mirrored = see_vectors_by_axis(owned)
     return 0.5 * (owned - jnp.swapaxes(mirrored, 1, 2))
 
 

time: 912 us -> 653 us (0.72)
  waiting for transfers between devices: 660 us -> 397 us
  blocking collectives: 26.7 us -> 36.5 us
    unnamed x2 -> x1, waiting for transfers between devices: 651 us -> 0.02 us
    reduce_scatter x0 -> x1, waiting for transfers between devices: none -> 388 us  [shards(): mine = lax.psum_scatter(stacked, 'sp', scatter_dimension=1, tiled=True)]
    dynamic_update_slice x24 -> x0, local copies, waits for them, and re-layouts: 21.6 us -> none  [shards(): _, stacked = lax.scan(project, jnp.zeros((), jnp.float32), velocity)]
    while x0 -> x1, local copies, waits for them, and re-layouts: none -> 17.9 us  [shards(): _, stacked = lax.scan(project, jnp.zeros((), jnp.float32), velocity)]
where the time goes in v1:
time: 653 us; the launch traced here: 652 us
  waiting for transfers between devices  397 us (61%)
  other arithmetic  93.1 us (14%)
  local copies, waits for them, and re-layouts  79.4 us (12%)
  blocking collectives  36.5 us (6%)
  matrix products  26.2 us (4%)
  between operations  13.8 us (2%)
    reduce_scatter x1, waiting for transfers between devices, shards(): mine = lax.psum_scatter(stacked, 'sp', scatter_dimension=1, tiled=True)  388 us
    convert_element_type x12, other arithmetic, project(): moved = moved.astype(jnp.bfloat16).reshape(-1, width)  88.8 us
    slice x24, local copies, waits for them, and re-layouts, project(): along_z = jnp.roll(centre, -1, axis=3) - jnp.roll(centre, 1, axis=3)  33.1 us
    all_to_all x1, blocking collectives, lax.all_to_all(jnp.stack(jnp.split(m, lax.axis_size('sp'), axis=2), axis=...  23.9 us
    dot_general x12, matrix products, project(): lax.dot_general(test_flat, moved, (((0,), (0,)), ((), ())), preferred_ele...  20.6 us
    dynamic_slice x12, local copies, waits for them, and re-layouts, shards(): _, stacked = lax.scan(project, jnp.zeros((), jnp.float32), velocity)  18.6 us
    while x1, local copies, waits for them, and re-layouts, shards(): _, stacked = lax.scan(project, jnp.zeros((), jnp.float32), velocity)  17.9 us
  transfers between devices with their start and end apart: 5, of which 4 were waited for; matrix products, arithmetic and copies ran while one was open for 1% of the time, Pallas kernels for 0%

profile of v1, /device:TPU:1, one launch (start us, length us, event | category | flops | bytes accessed | tf_op | source)
XLA Modules:
  0.0 652.1 jit_solution(13791874989647685911)
XLA Ops:
  6.5 1.1 fusion.12
  7.6 2.2 collective-permute-start
  9.9 4.2 collective-permute-done
  14.1 2.3 constant_dynamic-update-slice_fusion.1
  16.4 1.8 collective-permute-done.1
  18.3 1.8 copy-done.1
  20.1 1.0 fusion.11
  21.1 3.3 collective-permute-start.2
  24.4 5.6 fusion.6
  30.0 2.7 collective-permute-done.3
  32.7 3.4 pad_maximum_fusion
  36.0 161.7 %while.10 = (s32[]{:T(128)}, f32[12,256,256]{1,2,0:T(8,128)}, f32[12,3,8,16,16]{4,0,3,2,1:T(8,128)}, bf16[3,10,18,16,256]{4,3,2,1,0:T(8,128)(2,1)}, bf16[3,8,18,...) while((s32[]{:T(128)}, f32[12,256,256]{1,2,0:T(8,128)}, ...), condition=%wide.region_1.2_spmd, body=%wide.region_0.1_spmd.sunk | while | flops 830472192 | bytes 60154456 | solution.py:60
  36.0 1.5 constant_dynamic-slice_fusion.2
  37.6 1.9 fusion.25
  40.4 7.4 %fusion.26 = bf16[3,8,16,16,256]{4,3,2,1,0:T(8,128)(2,1)S(1)} fusion(f32[3,8,16,1,256]{4,3,2,1,0:T(1,128)S(1)} %get-tuple-element.160, f32[3,8,16,15,256]{4,3,2,1,0:T(8,128)S(1)} %get-tuple-element.161, f32[3,8,16,15,256]{4,3,2,1,0:T(8,128)S(1)} %get-tuple-element.162, f32[3,8,16,1,256]{4,3,2,1,0:T(1,128)S(1)} %get-tuple-element.163, ...), kind=kLoop, calls=%fused_computation.4.clone.1 | loop fusion | flops 25165824 | bytes 28336128 | tf_op jit(solution)/shard_map/while/body/eval_jaxpr/convert_element_type | solution.py:54
  47.8 1.7 fusion.27
  49.5 1.5 constant_dynamic-slice_fusion.2
  51.1 1.9 fusion.25
  53.9 7.4 %fusion.26 = bf16[3,8,16,16,256]{4,3,2,1,0:T(8,128)(2,1)S(1)} fusion(f32[3,8,16,1,256]{4,3,2,1,0:T(1,128)S(1)} %get-tuple-element.160, f32[3,8,16,15,256]{4,3,2,1,0:T(8,128)S(1)} %get-tuple-element.161, f32[3,8,16,15,256]{4,3,2,1,0:T(8,128)S(1)} %get-tuple-element.162, f32[3,8,16,1,256]{4,3,2,1,0:T(1,128)S(1)} %get-tuple-element.163, ...), kind=kLoop, calls=%fused_computation.4.clone.1 | loop fusion | flops 25165824 | bytes 28336128 | tf_op jit(solution)/shard_map/while/body/eval_jaxpr/convert_element_type | solution.py:54
  61.3 1.7 fusion.27
  63.0 1.5 constant_dynamic-slice_fusion.2
  64.6 1.9 fusion.25
  67.3 7.4 %fusion.26 = bf16[3,8,16,16,256]{4,3,2,1,0:T(8,128)(2,1)S(1)} fusion(f32[3,8,16,1,256]{4,3,2,1,0:T(1,128)S(1)} %get-tuple-element.160, f32[3,8,16,15,256]{4,3,2,1,0:T(8,128)S(1)} %get-tuple-element.161, f32[3,8,16,15,256]{4,3,2,1,0:T(8,128)S(1)} %get-tuple-element.162, f32[3,8,16,1,256]{4,3,2,1,0:T(1,128)S(1)} %get-tuple-element.163, ...), kind=kLoop, calls=%fused_computation.4.clone.1 | loop fusion | flops 25165824 | bytes 28336128 | tf_op jit(solution)/shard_map/while/body/eval_jaxpr/convert_element_type | solution.py:54
  74.7 1.7 fusion.27
  76.5 1.5 constant_dynamic-slice_fusion.2
  78.0 1.9 fusion.25
  80.8 7.4 %fusion.26 = bf16[3,8,16,16,256]{4,3,2,1,0:T(8,128)(2,1)S(1)} fusion(f32[3,8,16,1,256]{4,3,2,1,0:T(1,128)S(1)} %get-tuple-element.160, f32[3,8,16,15,256]{4,3,2,1,0:T(8,128)S(1)} %get-tuple-element.161, f32[3,8,16,15,256]{4,3,2,1,0:T(8,128)S(1)} %get-tuple-element.162, f32[3,8,16,1,256]{4,3,2,1,0:T(1,128)S(1)} %get-tuple-element.163, ...), kind=kLoop, calls=%fused_computation.4.clone.1 | loop fusion | flops 25165824 | bytes 28336128 | tf_op jit(solution)/shard_map/while/body/eval_jaxpr/convert_element_type | solution.py:54
  88.2 1.7 fusion.27
  90.0 1.5 constant_dynamic-slice_fusion.2
  91.5 1.9 fusion.25
  94.3 7.4 %fusion.26 = bf16[3,8,16,16,256]{4,3,2,1,0:T(8,128)(2,1)S(1)} fusion(f32[3,8,16,1,256]{4,3,2,1,0:T(1,128)S(1)} %get-tuple-element.160, f32[3,8,16,15,256]{4,3,2,1,0:T(8,128)S(1)} %get-tuple-element.161, f32[3,8,16,15,256]{4,3,2,1,0:T(8,128)S(1)} %get-tuple-element.162, f32[3,8,16,1,256]{4,3,2,1,0:T(1,128)S(1)} %get-tuple-element.163, ...), kind=kLoop, calls=%fused_computation.4.clone.1 | loop fusion | flops 25165824 | bytes 28336128 | tf_op jit(solution)/shard_map/while/body/eval_jaxpr/convert_element_type | solution.py:54
  101.7 1.7 fusion.27
  103.4 1.5 constant_dynamic-slice_fusion.2
  105.0 1.9 fusion.25
  107.8 7.4 %fusion.26 = bf16[3,8,16,16,256]{4,3,2,1,0:T(8,128)(2,1)S(1)} fusion(f32[3,8,16,1,256]{4,3,2,1,0:T(1,128)S(1)} %get-tuple-element.160, f32[3,8,16,15,256]{4,3,2,1,0:T(8,128)S(1)} %get-tuple-element.161, f32[3,8,16,15,256]{4,3,2,1,0:T(8,128)S(1)} %get-tuple-element.162, f32[3,8,16,1,256]{4,3,2,1,0:T(1,128)S(1)} %get-tuple-element.163, ...), kind=kLoop, calls=%fused_computation.4.clone.1 | loop fusion | flops 25165824 | bytes 28336128 | tf_op jit(solution)/shard_map/while/body/eval_jaxpr/convert_element_type | solution.py:54
  115.2 1.7 fusion.27
  116.9 1.5 constant_dynamic-slice_fusion.2
  118.5 1.9 fusion.25
  121.3 7.4 %fusion.26 = bf16[3,8,16,16,256]{4,3,2,1,0:T(8,128)(2,1)S(1)} fusion(f32[3,8,16,1,256]{4,3,2,1,0:T(1,128)S(1)} %get-tuple-element.160, f32[3,8,16,15,256]{4,3,2,1,0:T(8,128)S(1)} %get-tuple-element.161, f32[3,8,16,15,256]{4,3,2,1,0:T(8,128)S(1)} %get-tuple-element.162, f32[3,8,16,1,256]{4,3,2,1,0:T(1,128)S(1)} %get-tuple-element.163, ...), kind=kLoop, calls=%fused_computation.4.clone.1 | loop fusion | flops 25165824 | bytes 28336128 | tf_op jit(solution)/shard_map/while/body/eval_jaxpr/convert_element_type | solution.py:54
  128.7 1.7 fusion.27
  130.4 1.5 constant_dynamic-slice_fusion.2
  132.0 1.9 fusion.25
  134.7 7.4 %fusion.26 = bf16[3,8,16,16,256]{4,3,2,1,0:T(8,128)(2,1)S(1)} fusion(f32[3,8,16,1,256]{4,3,2,1,0:T(1,128)S(1)} %get-tuple-element.160, f32[3,8,16,15,256]{4,3,2,1,0:T(8,128)S(1)} %get-tuple-element.161, f32[3,8,16,15,256]{4,3,2,1,0:T(8,128)S(1)} %get-tuple-element.162, f32[3,8,16,1,256]{4,3,2,1,0:T(1,128)S(1)} %get-tuple-element.163, ...), kind=kLoop, calls=%fused_computation.4.clone.1 | loop fusion | flops 25165824 | bytes 28336128 | tf_op jit(solution)/shard_map/while/body/eval_jaxpr/convert_element_type | solution.py:54
  142.1 1.7 fusion.27
  143.9 1.5 constant_dynamic-slice_fusion.2
  145.4 1.9 fusion.25
  148.2 7.4 %fusion.26 = bf16[3,8,16,16,256]{4,3,2,1,0:T(8,128)(2,1)S(1)} fusion(f32[3,8,16,1,256]{4,3,2,1,0:T(1,128)S(1)} %get-tuple-element.160, f32[3,8,16,15,256]{4,3,2,1,0:T(8,128)S(1)} %get-tuple-element.161, f32[3,8,16,15,256]{4,3,2,1,0:T(8,128)S(1)} %get-tuple-element.162, f32[3,8,16,1,256]{4,3,2,1,0:T(1,128)S(1)} %get-tuple-element.163, ...), kind=kLoop, calls=%fused_computation.4.clone.1 | loop fusion | flops 25165824 | bytes 28336128 | tf_op jit(solution)/shard_map/while/body/eval_jaxpr/convert_element_type | solution.py:54
  155.6 1.7 fusion.27
  157.3 1.5 constant_dynamic-slice_fusion.2
  158.9 1.9 fusion.25
  161.7 7.4 %fusion.26 = bf16[3,8,16,16,256]{4,3,2,1,0:T(8,128)(2,1)S(1)} fusion(f32[3,8,16,1,256]{4,3,2,1,0:T(1,128)S(1)} %get-tuple-element.160, f32[3,8,16,15,256]{4,3,2,1,0:T(8,128)S(1)} %get-tuple-element.161, f32[3,8,16,15,256]{4,3,2,1,0:T(8,128)S(1)} %get-tuple-element.162, f32[3,8,16,1,256]{4,3,2,1,0:T(1,128)S(1)} %get-tuple-element.163, ...), kind=kLoop, calls=%fused_computation.4.clone.1 | loop fusion | flops 25165824 | bytes 28336128 | tf_op jit(solution)/shard_map/while/body/eval_jaxpr/convert_element_type | solution.py:54
  169.1 1.7 fusion.27
  170.8 1.5 constant_dynamic-slice_fusion.2
  172.4 1.9 fusion.25
  175.2 7.4 %fusion.26 = bf16[3,8,16,16,256]{4,3,2,1,0:T(8,128)(2,1)S(1)} fusion(f32[3,8,16,1,256]{4,3,2,1,0:T(1,128)S(1)} %get-tuple-element.160, f32[3,8,16,15,256]{4,3,2,1,0:T(8,128)S(1)} %get-tuple-element.161, f32[3,8,16,15,256]{4,3,2,1,0:T(8,128)S(1)} %get-tuple-element.162, f32[3,8,16,1,256]{4,3,2,1,0:T(1,128)S(1)} %get-tuple-element.163, ...), kind=kLoop, calls=%fused_computation.4.clone.1 | loop fusion | flops 25165824 | bytes 28336128 | tf_op jit(solution)/shard_map/while/body/eval_jaxpr/convert_element_type | solution.py:54
  182.6 1.7 fusion.27
  184.3 1.5 constant_dynamic-slice_fusion.2
  185.9 1.9 fusion.25
  188.7 7.4 %fusion.26 = bf16[3,8,16,16,256]{4,3,2,1,0:T(8,128)(2,1)S(1)} fusion(f32[3,8,16,1,256]{4,3,2,1,0:T(1,128)S(1)} %get-tuple-element.160, f32[3,8,16,15,256]{4,3,2,1,0:T(8,128)S(1)} %get-tuple-element.161, f32[3,8,16,15,256]{4,3,2,1,0:T(8,128)S(1)} %get-tuple-element.162, f32[3,8,16,1,256]{4,3,2,1,0:T(1,128)S(1)} %get-tuple-element.163, ...), kind=kLoop, calls=%fused_computation.4.clone.1 | loop fusion | flops 25165824 | bytes 28336128 | tf_op jit(solution)/shard_map/while/body/eval_jaxpr/convert_element_type | solution.py:54
  196.1 1.7 fusion.27
  197.8 17.9 %copy.217 = f32[12,256,256]{0,2,1:T(8,128)} copy(f32[12,256,256]{1,2,0:T(8,128)} %get-tuple-element.42) | data formatting | bytes 6291456 | tf_op jit(solution)/shard_map/while | solution.py:60
  215.7 388.3 %reduce-scatter.2.cloned.1.call-done = f32[12,4,256]{0,2,1:T(8,128)} async-done(((f32[12,256,256]{0,2,1:T(8,128)}), f32[12,4,256]{0,2,1:T(8,128)}) %reduce-scatter.2.cloned.1.call-update) | async-done | bytes 49168 | tf_op jit(solution)/shard_map/reduce_scatter | solution.py:61
  603.9 12.6 %psum.7 = f32[12,4,256]{0,2,1:T(8,128)S(1)} all-reduce(f32[12,4,256]{0,2,1:T(8,128)} %reduce-scatter.2.cloned.1.call-done), channel_id=1, replica_groups=mesh['grp'=2,'sp'=64] {'grp'}, use_global_device_ids=true, to_apply=%region_3.4 | all-reduce | flops 12288 | bytes 98304 | tf_op jit(solution)/shard_map/psum | solution.py:62
  618.3 23.9 %all_to_all.5 = f32[64,1,192]{2,1,0:T(1,128)S(1)} all-to-all(f32[64,1,192]{2,1,0:T(1,128)S(1)} %reshape.26), channel_id=1, replica_groups=mesh['grp'=2,'sp'=64] {'sp'}, dimensions={0} | all-to-all | bytes 98304 | tf_op jit(solution)/shard_map/all_to_all | solution.py:8
  (112 shorter events, 14.9 us)
Async XLA Ops:
  6.5 597.4 %reduce-scatter.2.cloned.1.call-start = ((), (), s32[]{:S(2)}) async-start(), calls=%async_computation.2 | async-start | bytes 34078720 | tf_op jit(solution)/shard_map/reduce_scatter | solution.py:61
  7.6 6.5 collective-permute-start
  9.8 8.5 %collective-permute-start.1 = (bf16[3,8,1,16,256]{4,3,2,1,0:T(8,128)(2,1)S(1)}, bf16[3,8,1,16,256]{4,3,2,1,0:T(8,128)(2,1)S(1)}, u32[]{:S(2)}, u32[]{:S(2)}) collective-permute-start(bf16[3,8,1,16,256]{4,3,2,1,0:T(8,128)(2,1)S(1)} %get-tuple-element.108), channel_id=1, source_target_pairs={{64,0},{0,64},{65,1},{1,65},{66,2},{2,66},{67,3},{3,67},{68,4},{4,... | collective-permute-start | bytes 589832 | tf_op jit(solution)/shard_map/ppermute | solution.py:27
  14.1 10.3 %copy-start = (bf16[3,8,16,16,256]{4,3,2,1,0:T(8,128)(2,1)S(1)}, bf16[3,8,16,16,256]{4,3,2,1,0:T(8,128)(2,1)}, u32[]{:S(2)}) copy-start(bf16[3,8,16,16,256]{4,3,2,1,0:T(8,128)(2,1)} %param.4) | copy-start | bytes 9437188
  14.1 10.2 %copy-start.3 = (s32[12]{0:T(128)S(1)}, s32[12]{0:T(128)}, u32[]{:S(2)}) copy-start(s32[12]{0:T(128)} %param.5) | copy-start | bytes 148
  18.3 1.8 copy-start.1
  21.1 8.9 %collective-permute-start.2 = (bf16[3,1,18,16,256]{4,3,2,1,0:T(8,128)(2,1)}, bf16[3,1,18,16,256]{4,3,2,1,0:T(8,128)(2,1)}, u32[]{:S(2)}, u32[]{:S(2)}) collective-permute-start(bf16[3,1,18,16,256]{4,3,2,1,0:T(8,128)(2,1)} %get-tuple-element.106), channel_id=1, source_target_pairs={{0,1},{1,2},{2,3},{3,4},{4,5},{5,6},{6,7},{7,8},{8,9},{9,10},{10,1... | collective-permute-start | bytes 1327112 | tf_op jit(solution)/shard_map/ppermute | solution.py:24
  24.3 8.3 %collective-permute-start.3 = (bf16[3,1,18,16,256]{4,3,2,1,0:T(8,128)(2,1)}, bf16[3,1,18,16,256]{4,3,2,1,0:T(8,128)(2,1)}, u32[]{:S(2)}, u32[]{:S(2)}) collective-permute-start(bf16[3,1,18,16,256]{4,3,2,1,0:T(8,128)(2,1)} %get-tuple-element.107), channel_id=1, source_target_pairs={{1,0},{2,1},{3,2},{4,3},{5,4},{6,5},{7,6},{8,7},{9,8},{10,9},{11,1... | collective-permute-start | bytes 1327112 | tf_op jit(solution)/shard_map/ppermute | solution.py:27
  24.3 8.3 %copy-start.2 = (bf16[3,8,18,16,256]{4,3,2,1,0:T(8,128)(2,1)S(1)}, bf16[3,8,18,16,256]{4,3,2,1,0:T(8,128)(2,1)}, u32[]{:S(2)}) copy-start(bf16[3,8,18,16,256]{4,3,2,1,0:T(8,128)(2,1)} %copy-done.1) | copy-start | bytes 10616836
Sparse Core Ops, SparseCore 0:
  215.8 388.1 reduce-scatter.1
